TPU v7x, 32 devices: a whole 2x2x4 slice. The times are simulated.
32 devices in a mesh: dp: 4 (over z), ctx: 8 (over y, x, core).
Axes of the slice: x: 2, y: 2, z: 4, core: 2. Of those that a mesh axis runs over, the one named last changes fastest.
Arguments:
- patches: bfloat16 [8, 1024, 6144], P('dp', 'ctx'), may hold values from -6 to 6
- w_in: bfloat16 [6144, 768], P(('dp', 'ctx')), may hold values from -0.078125 to 0.078125
- b_in: bfloat16 [768], P(('dp', 'ctx')), may hold values from -3 to 3
- g_one: bfloat16 [768], P(('dp', 'ctx')), may hold values from 0.25 to 1.75
- s_one: bfloat16 [768], P(('dp', 'ctx')), may hold values from -3 to 3
- w_qkv: bfloat16 [768, 2304], P(('dp', 'ctx')), may hold values from -0.21875 to 0.21875
- w_out: bfloat16 [768, 768], P(('dp', 'ctx')), may hold values from -1.75 to 1.75
- b_out: bfloat16 [768], P(('dp', 'ctx')), may hold values from -3 to 3
- g_two: bfloat16 [768], P(('dp', 'ctx')), may hold values from 0.25 to 1.75
- s_two: bfloat16 [768], P(('dp', 'ctx')), may hold values from -3 to 3
- w_up: bfloat16 [768, 3072], P(('dp', 'ctx')), may hold values from -0.21875 to 0.21875
- b_up: bfloat16 [3072], P(('dp', 'ctx')), may hold values from -3 to 3
- w_down: bfloat16 [3072, 768], P(('dp', 'ctx')), may hold values from -0.109375 to 0.109375
- b_down: bfloat16 [768], P(('dp', 'ctx')), may hold values from -3 to 3
- cotangent: bfloat16 [8, 1024, 768], P('dp', 'ctx'), may hold values from -6 to 6
Outputs:
- block_out: bfloat16 [8, 1024, 768], P('dp', 'ctx')
- grad_patches: float32 [8, 1024, 6144], P('dp', 'ctx')
- grad_w_in: float32 [6144, 768], P(('dp', 'ctx'))
- grad_b_in: float32 [768], P(('dp', 'ctx'))
- grad_g_one: float32 [768], P(('dp', 'ctx'))
- grad_s_one: float32 [768], P(('dp', 'ctx'))
- grad_w_qkv: float32 [768, 2304], P(('dp', 'ctx'))
- grad_w_out: float32 [768, 768], P(('dp', 'ctx'))
- grad_b_out: float32 [768], P(('dp', 'ctx'))
- grad_g_two: float32 [768], P(('dp', 'ctx'))
- grad_s_two: float32 [768], P(('dp', 'ctx'))
- grad_w_up: float32 [768, 3072], P(('dp', 'ctx'))
- grad_b_up: float32 [3072], P(('dp', 'ctx'))
- grad_w_down: float32 [3072, 768], P(('dp', 'ctx'))
- grad_b_down: float32 [768], P(('dp', 'ctx'))
All inputs are finite; a program needn't handle non-finite values.
Results may differ from a plain program's by a relative error of at most 0.015.
Values may be sent and summed in bfloat16 or wider, within the bound.
No kernel may reach another device: no remote copies, remote signals or barrier semaphores. Data moves between devices by JAX's collectives and lax.ppermute only.
A program may use at most 256 MiB of HBM per device.

v0:
```python
import jax
import jax.numpy as jnp
from jax import lax
from jax.sharding import PartitionSpec as P

HEADS = 12
HEAD = 64
eps_norm = 1e-05
gelu_coef = 0.7978845608028654


def norm_forward(stream, gain, shift):
    row_mean = jnp.mean(stream, axis=-1, keepdims=True)
    centered = stream - row_mean
    variance = jnp.mean(centered * centered, axis=-1, keepdims=True)
    inverse = lax.rsqrt(variance + eps_norm)
    normed = centered * inverse
    return (normed * gain + shift, normed, inverse)


def norm_backward(upstream, normed, inverse, gain):
    scaled = upstream * gain
    row_inner = jnp.mean(scaled, axis=-1, keepdims=True)
    row_corr = jnp.mean(scaled * normed, axis=-1, keepdims=True)
    stream_grad = inverse * (scaled - row_inner - normed * row_corr)
    return (stream_grad, jnp.sum(upstream * normed, axis=0), jnp.sum(upstream, axis=0))


def gelu_pair(pre_act):
    tanh_val = jnp.tanh(gelu_coef * (pre_act + 0.044715 * pre_act * pre_act * pre_act))
    gelu_out = 0.5 * pre_act * (1.0 + tanh_val)
    gelu_slope = 0.5 * (1.0 + tanh_val) + 0.5 * pre_act * (
        1.0 - tanh_val * tanh_val
    ) * gelu_coef * (1.0 + 3.0 * 0.044715 * pre_act * pre_act)
    return (gelu_out, gelu_slope)


def block_scores(queries, kv_all, key_block, key_width, offset):
    model_width = queries.shape[1] * queries.shape[2]
    kv_piece = lax.dynamic_slice_in_dim(kv_all, key_block * key_width, key_width, 0)
    key_rows = kv_piece[:, :model_width].reshape(key_width, HEADS, HEAD)
    value_rows = kv_piece[:, model_width:].reshape(key_width, HEADS, HEAD)
    scores = (
        jnp.einsum("qhd,khd->hqk", queries, key_rows, preferred_element_type=jnp.float32) * 0.125
    )
    key_pos = key_block * key_width + lax.iota(jnp.int32, key_width)
    row_pos = offset + lax.iota(jnp.int32, queries.shape[0])
    allowed = key_pos[None, :] <= row_pos[:, None]
    return (jnp.where(allowed[None], scores, -1e30), key_rows, value_rows)


def log_totals(queries, kv_all, key_width, offset, last_block):
    row_shape = (HEADS, queries.shape[0])

    def lse_step(key_block, state_pair):
        row_top, row_total = state_pair
        scores, key_rows, value_rows = block_scores(queries, kv_all, key_block, key_width, offset)
        new_top = jnp.maximum(row_top, jnp.max(scores, axis=-1))
        row_total = row_total * jnp.exp(row_top - new_top) + jnp.sum(
            jnp.exp(scores - new_top[..., None]), axis=-1
        )
        return (new_top, row_total)

    start_pair = (jnp.full(row_shape, -1e30, jnp.float32), jnp.zeros(row_shape, jnp.float32))
    row_top, row_total = lax.fori_loop(0, last_block, lse_step, start_pair)
    return row_top + jnp.log(row_total)


def attend_rows(queries, kv_all, row_lse, key_width, offset, last_block):

    def out_step(key_block, accumulated):
        scores, key_rows, value_rows = block_scores(queries, kv_all, key_block, key_width, offset)
        attn_probs = jnp.exp(scores - row_lse[..., None]).astype(jnp.bfloat16)
        return accumulated + jnp.einsum(
            "hqk,khd->qhd", attn_probs, value_rows, preferred_element_type=jnp.float32
        )

    accumulated = lax.fori_loop(0, last_block, out_step, jnp.zeros(queries.shape, jnp.float32))
    return accumulated.reshape(queries.shape[0], -1).astype(jnp.bfloat16)


def delta_rows(queries, kv_all, row_lse, grad_rows, key_width, offset, last_block):

    def delta_step(key_block, row_delta):
        scores, key_rows, value_rows = block_scores(queries, kv_all, key_block, key_width, offset)
        plain_probs = jnp.exp(scores - row_lse[..., None])
        prob_grad = jnp.einsum(
            "qhd,khd->hqk", grad_rows, value_rows, preferred_element_type=jnp.float32
        )
        return row_delta + jnp.sum(plain_probs * prob_grad, axis=-1)

    return lax.fori_loop(0, last_block, delta_step, jnp.zeros(row_lse.shape, jnp.float32))


def attend_back(
    queries, kv_all, row_lse, row_delta, grad_rows, key_width, offset, last_block, length
):
    model_width = queries.shape[1] * queries.shape[2]

    def grad_step(key_block, state_pair):
        query_grad, kv_grad = state_pair
        scores, key_rows, value_rows = block_scores(queries, kv_all, key_block, key_width, offset)
        plain_probs = jnp.exp(scores - row_lse[..., None])
        prob_grad = jnp.einsum(
            "qhd,khd->hqk", grad_rows, value_rows, preferred_element_type=jnp.float32
        )
        score_grad = (plain_probs * (prob_grad - row_delta[..., None])).astype(jnp.bfloat16)
        query_grad = query_grad + jnp.einsum(
            "hqk,khd->qhd", score_grad, key_rows, preferred_element_type=jnp.float32
        )
        key_grad = (
            jnp.einsum("hqk,qhd->khd", score_grad, queries, preferred_element_type=jnp.float32)
            * 0.125
        )
        value_grad = jnp.einsum(
            "hqk,qhd->khd",
            plain_probs.astype(jnp.bfloat16),
            grad_rows,
            preferred_element_type=jnp.float32,
        )
        kv_piece = jnp.concatenate(
            [key_grad.reshape(key_width, -1), value_grad.reshape(key_width, -1)], axis=1
        )
        kv_grad = lax.dynamic_update_slice_in_dim(kv_grad, kv_piece, key_block * key_width, 0)
        return (query_grad, kv_grad)

    start_pair = (
        jnp.zeros(queries.shape, jnp.float32),
        jnp.zeros((length, 2 * model_width), jnp.float32),
    )
    query_grad, kv_grad = lax.fori_loop(0, last_block, grad_step, start_pair)
    return (query_grad.reshape(queries.shape[0], -1) * 0.125, kv_grad)


def per_device(
    patches,
    w_in,
    b_in,
    g_one,
    s_one,
    w_qkv,
    w_out,
    b_out,
    g_two,
    s_two,
    w_up,
    b_up,
    w_down,
    b_down,
    cotangent,
):
    shards = (
        w_in,
        b_in,
        g_one,
        s_one,
        w_qkv,
        w_out,
        b_out,
        g_two,
        s_two,
        w_up,
        b_up,
        w_down,
        b_down,
    )
    micro_count = patches.shape[0]
    row_count = patches.shape[1]
    model_width = w_qkv.shape[1] // 3
    all_devices = lax.axis_size(("dp", "ctx"))
    length = row_count * lax.axis_size("ctx")
    key_width = min(512, length)
    offset = lax.axis_index("ctx") * row_count
    last_block = (offset + row_count - 1) // key_width + 1
    totals = [
        jnp.zeros((shard.shape[0] * all_devices,) + shard.shape[1:], jnp.float32)
        for shard in shards
    ]
    outputs = []
    in_grads = []
    for batch_index in range(micro_count):
        gathered = (
            lax.all_gather(w_in, ("dp", "ctx"), axis=0, tiled=True),
            lax.all_gather(b_in, ("dp", "ctx"), axis=0, tiled=True),
            lax.all_gather(g_one, ("dp", "ctx"), axis=0, tiled=True),
            lax.all_gather(s_one, ("dp", "ctx"), axis=0, tiled=True),
            lax.all_gather(w_qkv, ("dp", "ctx"), axis=0, tiled=True),
            lax.all_gather(w_out, ("dp", "ctx"), axis=0, tiled=True),
            lax.all_gather(b_out, ("dp", "ctx"), axis=0, tiled=True),
            lax.all_gather(g_two, ("dp", "ctx"), axis=0, tiled=True),
            lax.all_gather(s_two, ("dp", "ctx"), axis=0, tiled=True),
            lax.all_gather(w_up, ("dp", "ctx"), axis=0, tiled=True),
            lax.all_gather(b_up, ("dp", "ctx"), axis=0, tiled=True),
            lax.all_gather(w_down, ("dp", "ctx"), axis=0, tiled=True),
            lax.all_gather(b_down, ("dp", "ctx"), axis=0, tiled=True),
        )
        seq_patches = patches[batch_index]
        h_zero = jnp.dot(seq_patches, gathered[0], preferred_element_type=jnp.float32) + gathered[
            1
        ].astype(jnp.float32)
        gain_one = gathered[2].astype(jnp.float32)
        n_one, normed_one, inverse_one = norm_forward(
            h_zero, gain_one, gathered[3].astype(jnp.float32)
        )
        a_one = n_one.astype(jnp.bfloat16)
        projected = jnp.dot(a_one, gathered[4], preferred_element_type=jnp.float32).astype(
            jnp.bfloat16
        )
        queries = projected[:, :model_width].reshape(row_count, HEADS, HEAD)
        kv_all = lax.all_gather(projected[:, model_width:], "ctx", axis=0, tiled=True)
        row_lse = log_totals(queries, kv_all, key_width, offset, last_block)
        attended = attend_rows(queries, kv_all, row_lse, key_width, offset, last_block)
        h_one = (
            h_zero
            + jnp.dot(attended, gathered[5], preferred_element_type=jnp.float32)
            + gathered[6].astype(jnp.float32)
        )
        gain_two = gathered[7].astype(jnp.float32)
        n_two, normed_two, inverse_two = norm_forward(
            h_one, gain_two, gathered[8].astype(jnp.float32)
        )
        a_two = n_two.astype(jnp.bfloat16)
        pre_act = jnp.dot(a_two, gathered[9], preferred_element_type=jnp.float32) + gathered[
            10
        ].astype(jnp.float32)
        gelu_out, gelu_slope = gelu_pair(pre_act)
        hidden = gelu_out.astype(jnp.bfloat16)
        result = (
            h_one
            + jnp.dot(hidden, gathered[11], preferred_element_type=jnp.float32)
            + gathered[12].astype(jnp.float32)
        )
        outputs.append(result.astype(jnp.bfloat16))
        back_weights = (
            lax.all_gather(w_in, ("dp", "ctx"), axis=0, tiled=True),
            lax.all_gather(b_in, ("dp", "ctx"), axis=0, tiled=True),
            lax.all_gather(g_one, ("dp", "ctx"), axis=0, tiled=True),
            lax.all_gather(s_one, ("dp", "ctx"), axis=0, tiled=True),
            lax.all_gather(w_qkv, ("dp", "ctx"), axis=0, tiled=True),
            lax.all_gather(w_out, ("dp", "ctx"), axis=0, tiled=True),
            lax.all_gather(b_out, ("dp", "ctx"), axis=0, tiled=True),
            lax.all_gather(g_two, ("dp", "ctx"), axis=0, tiled=True),
            lax.all_gather(s_two, ("dp", "ctx"), axis=0, tiled=True),
            lax.all_gather(w_up, ("dp", "ctx"), axis=0, tiled=True),
            lax.all_gather(b_up, ("dp", "ctx"), axis=0, tiled=True),
            lax.all_gather(w_down, ("dp", "ctx"), axis=0, tiled=True),
            lax.all_gather(b_down, ("dp", "ctx"), axis=0, tiled=True),
        )
        seq_cot = cotangent[batch_index]
        cot_float = seq_cot.astype(jnp.float32)
        totals[12] = totals[12] + jnp.sum(cot_float, axis=0)
        totals[11] = totals[11] + jnp.dot(hidden.T, seq_cot, preferred_element_type=jnp.float32)
        pre_grad = (
            jnp.dot(seq_cot, back_weights[11].T, preferred_element_type=jnp.float32) * gelu_slope
        )
        totals[10] = totals[10] + jnp.sum(pre_grad, axis=0)
        up_grad = pre_grad.astype(jnp.bfloat16)
        totals[9] = totals[9] + jnp.dot(a_two.T, up_grad, preferred_element_type=jnp.float32)
        two_grad = jnp.dot(up_grad, back_weights[9].T, preferred_element_type=jnp.float32)
        norm_grad, gain_grad, shift_grad = norm_backward(
            two_grad, normed_two, inverse_two, back_weights[7].astype(jnp.float32)
        )
        totals[7] = totals[7] + gain_grad
        totals[8] = totals[8] + shift_grad
        stream_one = cot_float + norm_grad
        totals[6] = totals[6] + jnp.sum(stream_one, axis=0)
        out_grad = stream_one.astype(jnp.bfloat16)
        totals[5] = totals[5] + jnp.dot(attended.T, out_grad, preferred_element_type=jnp.float32)
        attended_grad = jnp.dot(
            out_grad, back_weights[5].T, preferred_element_type=jnp.float32
        ).astype(jnp.bfloat16)
        grad_rows = attended_grad.reshape(row_count, HEADS, HEAD)
        row_delta = delta_rows(queries, kv_all, row_lse, grad_rows, key_width, offset, last_block)
        query_grad, kv_terms = attend_back(
            queries, kv_all, row_lse, row_delta, grad_rows, key_width, offset, last_block, length
        )
        kv_local = lax.psum_scatter(
            kv_terms.astype(jnp.bfloat16), "ctx", scatter_dimension=0, tiled=True
        ).astype(jnp.float32)
        projected_grad = jnp.concatenate([query_grad, kv_local], axis=1).astype(jnp.bfloat16)
        totals[4] = totals[4] + jnp.dot(a_one.T, projected_grad, preferred_element_type=jnp.float32)
        one_grad = jnp.dot(projected_grad, back_weights[4].T, preferred_element_type=jnp.float32)
        norm_grad, gain_grad, shift_grad = norm_backward(
            one_grad, normed_one, inverse_one, back_weights[2].astype(jnp.float32)
        )
        totals[2] = totals[2] + gain_grad
        totals[3] = totals[3] + shift_grad
        stream_zero = stream_one + norm_grad
        totals[1] = totals[1] + jnp.sum(stream_zero, axis=0)
        zero_grad = stream_zero.astype(jnp.bfloat16)
        totals[0] = totals[0] + jnp.dot(
            seq_patches.T, zero_grad, preferred_element_type=jnp.float32
        )
        in_grads.append(jnp.dot(zero_grad, back_weights[0].T, preferred_element_type=jnp.float32))
    owned = (
        lax.psum_scatter(totals[0], ("dp", "ctx"), scatter_dimension=0, tiled=True),
        lax.psum_scatter(totals[1], ("dp", "ctx"), scatter_dimension=0, tiled=True),
        lax.psum_scatter(totals[2], ("dp", "ctx"), scatter_dimension=0, tiled=True),
        lax.psum_scatter(totals[3], ("dp", "ctx"), scatter_dimension=0, tiled=True),
        lax.psum_scatter(totals[4], ("dp", "ctx"), scatter_dimension=0, tiled=True),
        lax.psum_scatter(totals[5], ("dp", "ctx"), scatter_dimension=0, tiled=True),
        lax.psum_scatter(totals[6], ("dp", "ctx"), scatter_dimension=0, tiled=True),
        lax.psum_scatter(totals[7], ("dp", "ctx"), scatter_dimension=0, tiled=True),
        lax.psum_scatter(totals[8], ("dp", "ctx"), scatter_dimension=0, tiled=True),
        lax.psum_scatter(totals[9], ("dp", "ctx"), scatter_dimension=0, tiled=True),
        lax.psum_scatter(totals[10], ("dp", "ctx"), scatter_dimension=0, tiled=True),
        lax.psum_scatter(totals[11], ("dp", "ctx"), scatter_dimension=0, tiled=True),
        lax.psum_scatter(totals[12], ("dp", "ctx"), scatter_dimension=0, tiled=True),
    )
    return (jnp.stack(outputs), jnp.stack(in_grads)) + tuple(owned)


def solution(mesh):
    placed = (
        P("dp", "ctx", None),
        P(("dp", "ctx"), None),
        P(("dp", "ctx")),
        P(("dp", "ctx")),
        P(("dp", "ctx")),
        P(("dp", "ctx"), None),
        P(("dp", "ctx"), None),
        P(("dp", "ctx")),
        P(("dp", "ctx")),
        P(("dp", "ctx")),
        P(("dp", "ctx"), None),
        P(("dp", "ctx")),
        P(("dp", "ctx"), None),
        P(("dp", "ctx")),
        P("dp", "ctx", None),
    )
    return jax.shard_map(
        per_device,
        mesh=mesh,
        in_specs=placed,
        out_specs=(
            P("dp", "ctx", None),
            P("dp", "ctx", None),
            P(("dp", "ctx"), None),
            P(("dp", "ctx")),
            P(("dp", "ctx")),
            P(("dp", "ctx")),
            P(("dp", "ctx"), None),
            P(("dp", "ctx"), None),
            P(("dp", "ctx")),
            P(("dp", "ctx")),
            P(("dp", "ctx")),
            P(("dp", "ctx"), None),
            P(("dp", "ctx")),
            P(("dp", "ctx"), None),
            P(("dp", "ctx")),
        ),
        check_vma=False,
    )
```

profile of v0, /device:TPU:0, one launch (start us, length us, event | category | flops | bytes accessed | tf_op | source)
XLA Modules:
  0.0 1311.8 jit_solution(26952344656384240)
XLA Ops:
  15.4 42.9 %all-reduce.17 = (bf16[768]{0:T(1024)(128)(2,1)S(1)}, bf16[768]{0:T(1024)(128)(2,1)S(1)}, bf16[768]{0:T(1024)(128)(2,1)S(1)}, bf16[768]{0:T(1024)(128)(2,1)}, bf...) all-reduce(bf16[768]{0:T(1024)(128)(2,1)S(1)} %dynamic-update-slice, ...), channel_id=1, replica_groups=mesh['dp'=4,'ctx'=8] {'dp','ctx'}, use_global_device_ids=true, to_apply=%add | all-reduce | flops 8448 | bytes 33792
  58.3 37.5 %all-gather.8.cloned.1.call-done = bf16[6144,768]{1,0:T(8,128)(2,1)} async-done(((bf16[192,768]{1,0:T(8,128)(2,1)}), bf16[6144,768]{1,0:T(8,128)(2,1)}) %all-gather.8.cloned.1.call-update) | async-done | bytes 9437200 | tf_op jit(solution)/shard_map/all_gather | solution.py:183
  101.7 55.7 %all-gather.10.cloned.1.call-done = bf16[768,2304]{1,0:T(8,128)(2,1)} async-done(((bf16[24,2304]{1,0:T(8,128)(2,1)}), bf16[768,2304]{1,0:T(8,128)(2,1)}) %all-gather.10.cloned.1.call-update) | async-done | bytes 3538960 | tf_op jit(solution)/shard_map/all_gather | solution.py:187
  161.7 5.8 fusion.125
  177.6 15.4 %all-gather.12.cloned.1.call-done = bf16[1024,1536]{1,0:T(8,128)(2,1)} async-done(((bf16[128,1536]{1,0:T(8,128)(2,1)}), bf16[1024,1536]{1,0:T(8,128)(2,1)}) %all-gather.12.cloned.1.call-update) | async-done | bytes 3145744 | tf_op jit(solution)/shard_map/all_gather | solution.py:210
  208.5 18.6 %all-gather.20.cloned.1.call-done = bf16[1024,1536]{1,0:T(8,128)(2,1)} async-done(((bf16[128,1536]{1,0:T(8,128)(2,1)}), bf16[1024,1536]{1,0:T(8,128)(2,1)}) %all-gather.20.cloned.1.call-update) | async-done | bytes 3145744 | tf_op jit(solution)/shard_map/all_gather | solution.py:210
  238.1 7.0 while.91
  246.8 37.1 %all-gather.14.cloned.1.call-done = bf16[768,768]{1,0:T(8,128)(2,1)} async-done(((bf16[24,768]{1,0:T(8,128)(2,1)}), bf16[768,768]{1,0:T(8,128)(2,1)}) %all-gather.14.cloned.1.call-update) | async-done | bytes 1179664 | tf_op jit(solution)/shard_map/all_gather | solution.py:188
  289.6 59.6 %all-gather.16.cloned.1.call-done = bf16[768,3072]{1,0:T(8,128)(2,1)} async-done(((bf16[24,3072]{1,0:T(8,128)(2,1)}), bf16[768,3072]{1,0:T(8,128)(2,1)}) %all-gather.16.cloned.1.call-update) | async-done | bytes 4718608 | tf_op jit(solution)/shard_map/all_gather | solution.py:192
  353.7 60.9 %all-gather.18.cloned.1.call-done = bf16[3072,768]{1,0:T(8,128)(2,1)} async-done(((bf16[96,768]{1,0:T(8,128)(2,1)}), bf16[3072,768]{1,0:T(8,128)(2,1)}) %all-gather.18.cloned.1.call-update) | async-done | bytes 4718608 | tf_op jit(solution)/shard_map/all_gather | solution.py:194
  442.6 11.3 while.92
  456.8 7.4 while.93
  471.9 7.4 while.95
  504.2 23.9 %reduce-scatter.22.cloned.1.call-done = bf16[128,1536]{1,0:T(8,128)(2,1)} async-done(((bf16[1024,1536]{1,0:T(8,128)(2,1)}), bf16[128,1536]{1,0:T(8,128)(2,1)}) %reduce-scatter.22.cloned.1.call-update) | async-done | bytes 393232
  529.3 49.4 %reduce-scatter.24.cloned.1.call-done = bf16[128,1536]{1,0:T(8,128)(2,1)} async-done(((bf16[1024,1536]{1,0:T(8,128)(2,1)}), bf16[128,1536]{1,0:T(8,128)(2,1)}) %reduce-scatter.24.cloned.1.call-update) | async-done | bytes 393232
  593.0 8.1 fusion.63
  601.1 12.6 add_bitcast_fusion
  613.7 18.7 %copy.109 = f32[6144,768]{1,0:T(8,128)} copy(f32[6144,768]{0,1:T(8,128)} %add_bitcast_fusion) | data formatting | bytes 37748736
  642.0 40.9 %all-reduce.16 = (f32[768]{0:T(1024)S(1)}, f32[768]{0:T(1024)S(1)}, f32[768]{0:T(1024)S(1)}, f32[768]{0:T(1024)S(1)}, f32[768]{0:T(1024)S(1)}, /*index=5*/f32[76...) all-reduce(f32[768]{0:T(1024)S(1)} %add.529, ...), channel_id=5, replica_groups=mesh['dp'=4,'ctx'=8] {'dp','ctx'}, use_global_device_ids=true, to_apply=%region_43.44.clone | all-reduce | flops 8448 | bytes 67584
  687.6 6.9 convolution_bitcast_fusion.2
  700.8 125.0 %reduce-scatter.20.cloned.1.call-done = f32[96,768]{1,0:T(8,128)} async-done(((f32[3072,768]{1,0:T(8,128)}), f32[96,768]{1,0:T(8,128)}) %reduce-scatter.20.cloned.1.call-update) | async-done | bytes 294928 | tf_op jit(solution)/shard_map/reduce_scatter | solution.py:307
  825.8 140.9 %reduce-scatter.18.cloned.1.call-done = f32[24,3072]{1,0:T(8,128)} async-done(((f32[768,3072]{1,0:T(8,128)}), f32[24,3072]{1,0:T(8,128)}) %reduce-scatter.18.cloned.1.call-update) | async-done | bytes 294928 | tf_op jit(solution)/shard_map/reduce_scatter | solution.py:305
  966.7 125.3 %reduce-scatter.14.cloned.1.call-done = f32[24,2304]{1,0:T(8,128)} async-done(((f32[768,2304]{1,0:T(8,128)}), f32[24,2304]{1,0:T(8,128)}) %reduce-scatter.14.cloned.1.call-update) | async-done | bytes 221200 | tf_op jit(solution)/shard_map/reduce_scatter | solution.py:300
  1092.0 212.8 %reduce-scatter.26.cloned.1.call-done = f32[192,768]{1,0:T(8,128)} async-done(((f32[6144,768]{1,0:T(8,128)}), f32[192,768]{1,0:T(8,128)}) %reduce-scatter.26.cloned.1.call-update) | async-done | bytes 589840
  (455 shorter events, 204.3 us)
Async XLA Ops:
  7.2 88.6 %all-gather.8.cloned.1.call-start = ((), (), s32[]{:S(2)}) async-start(), calls=%async_computation.7 | async-start | bytes 9732096 | tf_op jit(solution)/shard_map/all_gather | solution.py:183
  7.9 149.5 %all-gather.10.cloned.1.call-start = ((), (), s32[]{:S(2)}) async-start(), calls=%async_computation.8 | async-start | bytes 3649536 | tf_op jit(solution)/shard_map/all_gather | solution.py:187
  8.7 184.3 %all-gather.12.cloned.1.call-start = ((), (), s32[]{:S(2)}) async-start(), calls=%async_computation.9 | async-start | bytes 3538944 | tf_op jit(solution)/shard_map/all_gather | solution.py:210
  58.3 109.4 %copy-start.59 = (f32[768]{0:T(1024)}, f32[768]{0:T(1024)S(1)}, u32[]{:S(2)}) copy-start(f32[768]{0:T(1024)S(1)} %convert_element_type.137) | copy-start | bytes 9220
  58.3 109.4 %copy-start.68 = (f32[768]{0:T(1024)}, f32[768]{0:T(1024)S(1)}, u32[]{:S(2)}) copy-start(f32[768]{0:T(1024)S(1)} %convert_element_type.138) | copy-start | bytes 9220
  161.7 65.4 %all-gather.20.cloned.1.call-start = ((), (), s32[]{:S(2)}) async-start(), calls=%async_computation.13 | async-start | bytes 3538944 | tf_op jit(solution)/shard_map/all_gather | solution.py:210
  170.2 113.7 %all-gather.14.cloned.1.call-start = ((), (), s32[]{:S(2)}) async-start(), calls=%async_computation.10 | async-start | bytes 1216512 | tf_op jit(solution)/shard_map/all_gather | solution.py:188
  170.7 178.5 %all-gather.16.cloned.1.call-start = ((), (), s32[]{:S(2)}) async-start(), calls=%async_computation.11 | async-start | bytes 4866048 | tf_op jit(solution)/shard_map/all_gather | solution.py:192
  171.3 243.3 %all-gather.18.cloned.1.call-start = ((), (), s32[]{:S(2)}) async-start(), calls=%async_computation.12 | async-start | bytes 4866048 | tf_op jit(solution)/shard_map/all_gather | solution.py:194
  172.1 356.0 %reduce-scatter.22.cloned.1.call-start = ((), (), s32[]{:S(2)}) async-start(), calls=%async_computation.18 | async-start | bytes 3538944
  285.9 142.7 %copy-start.76 = (f32[128]{0:T(128)}, f32[128]{0:T(128)S(1)}, u32[]{:S(2)}) copy-start(f32[128]{0:T(128)S(1)} %broadcast_multiply_fusion.10) | copy-start | bytes 1540
  287.7 140.9 %copy-start.86 = (f32[128]{0:T(128)}, f32[128]{0:T(128)S(1)}, u32[]{:S(2)}) copy-start(f32[128]{0:T(128)S(1)} %broadcast_multiply_fusion.8) | copy-start | bytes 1540
  469.0 109.7 %reduce-scatter.24.cloned.1.call-start = ((), (), s32[]{:S(2)}) async-start(), calls=%async_computation.19 | async-start | bytes 3538944
  484.0 216.8 %reduce-scatter.16.cloned.1.call-start = ((), (), s32[]{:S(2)}) async-start(), calls=%async_computation.15 | async-start | bytes 2433024 | tf_op jit(solution)/shard_map/reduce_scatter | solution.py:301
  487.6 338.2 %reduce-scatter.20.cloned.1.call-start = ((), (), s32[]{:S(2)}) async-start(), calls=%async_computation.17 | async-start | bytes 9732096 | tf_op jit(solution)/shard_map/reduce_scatter | solution.py:307
  495.0 471.7 %reduce-scatter.18.cloned.1.call-start = ((), (), s32[]{:S(2)}) async-start(), calls=%async_computation.16 | async-start | bytes 9732096 | tf_op jit(solution)/shard_map/reduce_scatter | solution.py:305
  502.8 77.1 %copy-start.60 = (f32[768]{0:T(1024)S(1)}, f32[768]{0:T(1024)}, u32[]{:S(2)}) copy-start(f32[768]{0:T(1024)} %copy-done.59) | copy-start | bytes 9220
  502.8 77.1 %copy-start.69 = (f32[768]{0:T(1024)S(1)}, f32[768]{0:T(1024)}, u32[]{:S(2)}) copy-start(f32[768]{0:T(1024)} %copy-done.68) | copy-start | bytes 9220
  502.8 77.1 %copy-start.94 = (f32[128]{0:T(128)S(1)}, f32[128]{0:T(128)}, u32[]{:S(2)}) copy-start(f32[128]{0:T(128)} %copy-done.93) | copy-start | bytes 1540
  502.8 77.1 %copy-start.109 = (f32[128]{0:T(128)S(1)}, f32[128]{0:T(128)}, u32[]{:S(2)}) copy-start(f32[128]{0:T(128)} %copy-done.108) | copy-start | bytes 1540
  502.9 77.1 %copy-start.17 = (f32[128,768]{1,0:T(8,128)S(1)}, f32[128,768]{1,0:T(8,128)}, u32[]{:S(2)}) copy-start(f32[128,768]{1,0:T(8,128)} %copy-done.16) | copy-start | bytes 1179652
  502.9 589.1 %reduce-scatter.14.cloned.1.call-start = ((), (), s32[]{:S(2)}) async-start(), calls=%async_computation.14 | async-start | bytes 7299072 | tf_op jit(solution)/shard_map/reduce_scatter | solution.py:300
  504.0 77.3 %copy-start.58 = (bf16[128,12,64]{0,2,1:T(8,128)(2,1)}, bf16[128,12,64]{0,2,1:T(8,128)(2,1)S(1)}, u32[]{:S(2)}) copy-start(bf16[128,12,64]{0,2,1:T(8,128)(2,1)S(1)} %multiply_convert_fusion.3) | copy-start | bytes 589828
  585.5 719.4 %reduce-scatter.26.cloned.1.call-start = ((), (), s32[]{:S(2)}) async-start(), calls=%async_computation.20 | async-start | bytes 19464192
  (109 other events, 629.8 us)
Sparse Core Ops, SparseCore 0:
  10.9 84.8 all-gather.7
  98.7 58.6 all-gather.9
  161.8 31.1 all-gather.11
  194.7 32.3 all-gather.19
  229.8 54.0 all-gather.13
  286.6 62.5 all-gather.15
  352.1 62.4 all-gather.17
  469.1 58.9 reduce-scatter.21
  532.4 46.2 reduce-scatter.23
  584.4 99.1 reduce-scatter.15
  691.0 134.6 reduce-scatter.19
  832.1 134.5 reduce-scatter.17
  973.9 118.0 reduce-scatter.13
  1098.8 205.9 reduce-scatter.25
where the time goes:
time: 1320 us; the launch traced here: 1310 us
  waiting for transfers between devices  965 us (73%)
  matrix products  124 us (9%)
  local copies, waits for them, and re-layouts  91.7 us (7%)
  blocking collectives  83.8 us (6%)
  other arithmetic  21.3 us (2%)
  between operations  15.7 us (1%)
    unnamed x17, waiting for transfers between devices  289 us
    reduce_scatter x1, waiting for transfers between devices, per_device(): lax.psum_scatter(totals[9], ('dp', 'ctx'), scatter_dimension=0, tiled=True)  141 us
    reduce_scatter x1, waiting for transfers between devices, per_device(): lax.psum_scatter(totals[4], ('dp', 'ctx'), scatter_dimension=0, tiled=True)  125 us
    reduce_scatter x1, waiting for transfers between devices, per_device(): lax.psum_scatter(totals[11], ('dp', 'ctx'), scatter_dimension=0, tiled=True)  125 us
    unnamed x2, blocking collectives  83.8 us
    all_gather x1, waiting for transfers between devices, per_device(): lax.all_gather(w_down, ('dp', 'ctx'), axis=0, tiled=True)  60.9 us
    all_gather x1, waiting for transfers between devices, per_device(): lax.all_gather(w_up, ('dp', 'ctx'), axis=0, tiled=True)  59.6 us
    all_gather x1, waiting for transfers between devices, per_device(): lax.all_gather(w_qkv, ('dp', 'ctx'), axis=0, tiled=True)  55.7 us
  transfers between devices with their start and end apart: 14, of which 13 were waited for; matrix products, arithmetic and copies ran while one was open for 13% of the time, Pallas kernels for 0%

commit v1 on v0

--- a/solution.py
+++ b/solution.py
@@ -7,6 +7,19 @@
 HEAD = 64
 eps_norm = 1e-05
 gelu_coef = 0.7978845608028654
+
+
+def gather_around(x, axis, dim):
+    ways = lax.axis_size(axis)
+    up = [(d, (d + 1) % ways) for d in range(ways)]
+    down = [(d, (d - 1) % ways) for d in range(ways)]
+    earlier, later = ([x], [x])
+    for _ in range(ways // 2):
+        earlier.append(lax.ppermute(earlier[-1], axis, up))
+    for _ in range((ways - 1) // 2):
+        later.append(lax.ppermute(later[-1], axis, down))
+    line = jnp.concatenate([*earlier[::-1], *later[1:]], axis=dim)
+    return jnp.roll(line, (lax.axis_index(axis) - ways // 2) * x.shape[dim], axis=dim)
 
 
 def norm_forward(stream, gain, shift):
@@ -207,7 +220,7 @@
             jnp.bfloat16
         )
         queries = projected[:, :model_width].reshape(row_count, HEADS, HEAD)
-        kv_all = lax.all_gather(projected[:, model_width:], "ctx", axis=0, tiled=True)
+        kv_all = gather_around(projected[:, model_width:], "ctx", 0)
         row_lse = log_totals(queries, kv_all, key_width, offset, last_block)
         attended = attend_rows(queries, kv_all, row_lse, key_width, offset, last_block)
         h_one = (

time: 1320 us -> 1250 us (0.947)
  waiting for transfers between devices: 965 us -> 873 us
  starting transfers between devices: 1.03 us -> 15.4 us
    all_gather x1, waiting for transfers between devices: 59.6 us -> 0.01 us  [per_device(): lax.all_gather(w_up, ('dp', 'ctx'), axis=0, tiled=True)]
    ppermute x0 -> x14, waiting for transfers between devices: none -> 43.8 us  [the longest x8 42.4 us: gather_around(): earlier.append(lax.ppermute(earlier[-1], axis, up))]
    all_gather x1, waiting for transfers between devices: 37.1 us -> 0.01 us  [per_device(): lax.all_gather(w_out, ('dp', 'ctx'), axis=0, tiled=True)]
    all_gather x2 -> x0, waiting for transfers between devices: 33.9 us -> none  [per_device(): lax.all_gather(projected[:, model_width:], 'ctx', axis=0, tiled=True)]
    ppermute x0 -> x14, starting transfers between devices: none -> 14.5 us  [the longest x6 12.4 us: gather_around(): later.append(lax.ppermute(later[-1], axis, down))]
    unnamed x219 -> x249, local copies, waits for them, and re-layouts: 53 us -> 60.7 us
    unnamed x17 -> x15, waiting for transfers between devices: 289 us -> 289 us
  transfers between devices with their start and end apart: 14 -> 26, of which waited for: 13 -> 17; matrix products, arithmetic and copies ran while one was open for 13% -> 15% of each run, Pallas kernels for 0% -> 0%
where the time goes in v1:
time: 1250 us; the launch traced here: 1240 us
  waiting for transfers between devices  873 us (70%)
  matrix products  124 us (10%)
  local copies, waits for them, and re-layouts  97.5 us (8%)
  blocking collectives  83.8 us (7%)
  other arithmetic  26 us (2%)
  between operations  16.3 us (1%)
  starting transfers between devices  15.4 us (1%)
    unnamed x15, waiting for transfers between devices  289 us
    reduce_scatter x1, waiting for transfers between devices, per_device(): lax.psum_scatter(totals[9], ('dp', 'ctx'), scatter_dimension=0, tiled=True)  141 us
    reduce_scatter x1, waiting for transfers between devices, per_device(): lax.psum_scatter(totals[4], ('dp', 'ctx'), scatter_dimension=0, tiled=True)  126 us
    reduce_scatter x1, waiting for transfers between devices, per_device(): lax.psum_scatter(totals[11], ('dp', 'ctx'), scatter_dimension=0, tiled=True)  125 us
    unnamed x2, blocking collectives  83.8 us
    unnamed x249, local copies, waits for them, and re-layouts  60.7 us
    all_gather x1, waiting for transfers between devices, per_device(): lax.all_gather(w_down, ('dp', 'ctx'), axis=0, tiled=True)  57.5 us
    all_gather x1, waiting for transfers between devices, per_device(): lax.all_gather(w_qkv, ('dp', 'ctx'), axis=0, tiled=True)  55.2 us
  transfers between devices with their start and end apart: 26, of which 17 were waited for; matrix products, arithmetic and copies ran while one was open for 15% of the time, Pallas kernels for 0%

profile of v1, /device:TPU:0, one launch (start us, length us, event | category | flops | bytes accessed | tf_op | source)
XLA Modules:
  0.0 1236.8 jit_solution(15776163148886046769)
XLA Ops:
  16.8 42.9 %all-reduce.17 = (bf16[768]{0:T(1024)(128)(2,1)S(1)}, bf16[768]{0:T(1024)(128)(2,1)S(1)}, bf16[768]{0:T(1024)(128)(2,1)S(1)}, bf16[768]{0:T(1024)(128)(2,1)}, bf...) all-reduce(bf16[768]{0:T(1024)(128)(2,1)S(1)} %dynamic-update-slice, ...), channel_id=1, replica_groups=mesh['dp'=4,'ctx'=8] {'dp','ctx'}, use_global_device_ids=true, to_apply=%add | all-reduce | flops 8448 | bytes 33792
  59.7 35.8 %all-gather.6.cloned.1.call-done = bf16[6144,768]{1,0:T(8,128)(2,1)} async-done(((bf16[192,768]{1,0:T(8,128)(2,1)}), bf16[6144,768]{1,0:T(8,128)(2,1)}) %all-gather.6.cloned.1.call-update) | async-done | bytes 9437200 | tf_op jit(solution)/shard_map/all_gather | solution.py:196
  101.9 55.2 %all-gather.8.cloned.1.call-done = bf16[768,2304]{1,0:T(8,128)(2,1)} async-done(((bf16[24,2304]{1,0:T(8,128)(2,1)}), bf16[768,2304]{1,0:T(8,128)(2,1)}) %all-gather.8.cloned.1.call-update) | async-done | bytes 3538960 | tf_op jit(solution)/shard_map/all_gather | solution.py:200
  172.0 6.4 collective-permute-done
  178.4 8.6 collective-permute-done.8
  196.4 10.0 collective-permute-done.9
  215.5 8.2 collective-permute-done.10
  235.4 6.7 fusion.50
  268.7 7.4 while.89
  288.1 57.5 %all-gather.14.cloned.1.call-done = bf16[3072,768]{1,0:T(8,128)(2,1)} async-done(((bf16[96,768]{1,0:T(8,128)(2,1)}), bf16[3072,768]{1,0:T(8,128)(2,1)}) %all-gather.14.cloned.1.call-update) | async-done | bytes 4718608 | tf_op jit(solution)/shard_map/all_gather | solution.py:207
  379.5 8.6 while.93
  395.8 7.4 while.95
  413.3 5.7 convolution_add_fusion.1
  428.0 25.1 %reduce-scatter.22.cloned.1.call-done = bf16[128,1536]{1,0:T(8,128)(2,1)} async-done(((bf16[1024,1536]{1,0:T(8,128)(2,1)}), bf16[128,1536]{1,0:T(8,128)(2,1)}) %reduce-scatter.22.cloned.1.call-update) | async-done | bytes 393232
  454.4 48.8 %reduce-scatter.24.cloned.1.call-done = bf16[128,1536]{1,0:T(8,128)(2,1)} async-done(((bf16[1024,1536]{1,0:T(8,128)(2,1)}), bf16[128,1536]{1,0:T(8,128)(2,1)}) %reduce-scatter.24.cloned.1.call-update) | async-done | bytes 393232
  517.5 8.0 fusion.65
  525.6 12.5 %add_bitcast_fusion = f32[6144,768]{0,1:T(8,128)} fusion(f32[768,6144]{1,0:T(8,128)} %fusion.65, bf16[2,128,6144]{2,1,0:T(8,128)(2,1)S(1)} %copy-done.4, bf16[128,768]{1,0:T(8,128)(2,1)S(1)} %get-tuple-element.780), kind=kOutput, calls=%fused_computation.102 | convolution fusion | flops 1212678144 | bytes 39518208 | tf_op jit(solution)/shard_map/dot_general | solution.py:304
  538.0 18.7 %copy.109 = f32[6144,768]{1,0:T(8,128)} copy(f32[6144,768]{0,1:T(8,128)} %add_bitcast_fusion) | data formatting | bytes 37748736
  566.4 40.8 %all-reduce.16 = (f32[768]{0:T(1024)S(1)}, f32[768]{0:T(1024)S(1)}, f32[768]{0:T(1024)S(1)}, f32[768]{0:T(1024)S(1)}, f32[768]{0:T(1024)S(1)}, /*index=5*/f32[76...) all-reduce(f32[768]{0:T(1024)S(1)} %add.538, ...), channel_id=5, replica_groups=mesh['dp'=4,'ctx'=8] {'dp','ctx'}, use_global_device_ids=true, to_apply=%region_43.45.clone | all-reduce | flops 8448 | bytes 67584
  611.9 6.9 convolution_bitcast_fusion.2
  625.1 125.2 %reduce-scatter.20.cloned.1.call-done = f32[96,768]{1,0:T(8,128)} async-done(((f32[3072,768]{1,0:T(8,128)}), f32[96,768]{1,0:T(8,128)}) %reduce-scatter.20.cloned.1.call-update) | async-done | bytes 294928 | tf_op jit(solution)/shard_map/reduce_scatter | solution.py:320
  750.3 140.7 %reduce-scatter.18.cloned.1.call-done = f32[24,3072]{1,0:T(8,128)} async-done(((f32[768,3072]{1,0:T(8,128)}), f32[24,3072]{1,0:T(8,128)}) %reduce-scatter.18.cloned.1.call-update) | async-done | bytes 294928 | tf_op jit(solution)/shard_map/reduce_scatter | solution.py:318
  891.0 125.6 %reduce-scatter.14.cloned.1.call-done = f32[24,2304]{1,0:T(8,128)} async-done(((f32[768,2304]{1,0:T(8,128)}), f32[24,2304]{1,0:T(8,128)}) %reduce-scatter.14.cloned.1.call-update) | async-done | bytes 221200 | tf_op jit(solution)/shard_map/reduce_scatter | solution.py:313
  1016.6 212.9 %reduce-scatter.26.cloned.1.call-done = f32[192,768]{1,0:T(8,128)} async-done(((f32[6144,768]{1,0:T(8,128)}), f32[192,768]{1,0:T(8,128)}) %reduce-scatter.26.cloned.1.call-update) | async-done | bytes 589840
  (513 shorter events, 235.2 us)
Async XLA Ops:
  7.2 88.3 %all-gather.6.cloned.1.call-start = ((), (), s32[]{:S(2)}) async-start(), calls=%async_computation.7 | async-start | bytes 9732096 | tf_op jit(solution)/shard_map/all_gather | solution.py:196
  7.9 149.2 %all-gather.8.cloned.1.call-start = ((), (), s32[]{:S(2)}) async-start(), calls=%async_computation.8 | async-start | bytes 3649536 | tf_op jit(solution)/shard_map/all_gather | solution.py:200
  8.7 269.1 %all-gather.10.cloned.1.call-start = ((), (), s32[]{:S(2)}) async-start(), calls=%async_computation.9 | async-start | bytes 1216512 | tf_op jit(solution)/shard_map/all_gather | solution.py:201
  9.4 274.2 %all-gather.12.cloned.1.call-start = ((), (), s32[]{:S(2)}) async-start(), calls=%async_computation.10 | async-start | bytes 4866048 | tf_op jit(solution)/shard_map/all_gather | solution.py:205
  10.0 335.6 %all-gather.14.cloned.1.call-start = ((), (), s32[]{:S(2)}) async-start(), calls=%async_computation.11 | async-start | bytes 4866048 | tf_op jit(solution)/shard_map/all_gather | solution.py:207
  169.3 17.7 %collective-permute-start.8 = (bf16[128,1536]{1,0:T(8,128)(2,1)S(1)}, bf16[128,1536]{1,0:T(8,128)(2,1)S(1)}, u32[]{:S(2)}, u32[]{:S(2)}) collective-permute-start(bf16[128,1536]{1,0:T(8,128)(2,1)S(1)} %collective-permute-done.7), channel_id=1, source_target_pairs={{0,1},{1,2},{2,3},{3,4},{4,5},{5,6},{6,7},{7,0},{8,9},{9,10},{10,1... | collective-permute-start | bytes 1179656 | tf_op jit(solution)/shard_map/ppermute | solution.py:18
  169.7 17.3 %collective-permute-start.4 = (bf16[128,1536]{1,0:T(8,128)(2,1)S(1)}, bf16[128,1536]{1,0:T(8,128)(2,1)S(1)}, u32[]{:S(2)}, u32[]{:S(2)}) collective-permute-start(bf16[128,1536]{1,0:T(8,128)(2,1)S(1)} %slice.74), channel_id=1, source_target_pairs={{0,7},{1,0},{2,1},{3,2},{4,3},{5,4},{6,5},{7,6},{8,15},{9,8},{10,9... | collective-permute-start | bytes 1179656 | tf_op jit(solution)/shard_map/ppermute | solution.py:20
  171.9 19.1 %collective-permute-start.11 = (bf16[128,1536]{1,0:T(8,128)(2,1)S(1)}, bf16[128,1536]{1,0:T(8,128)(2,1)S(1)}, u32[]{:S(2)}, u32[]{:S(2)}) collective-permute-start(bf16[128,1536]{1,0:T(8,128)(2,1)S(1)} %slice.76), channel_id=1, source_target_pairs={{0,7},{1,0},{2,1},{3,2},{4,3},{5,4},{6,5},{7,6},{8,15},{9,8},{10,9... | collective-permute-start | bytes 1179656 | tf_op jit(solution)/shard_map/ppermute | solution.py:20
  178.4 18.0 %collective-permute-start.1 = (bf16[128,1536]{1,0:T(8,128)(2,1)S(1)}, bf16[128,1536]{1,0:T(8,128)(2,1)}, u32[]{:S(2)}, u32[]{:S(2)}) collective-permute-start(bf16[128,1536]{1,0:T(8,128)(2,1)S(1)} %collective-permute-done), channel_id=1, source_target_pairs={{0,1},{1,2},{2,3},{3,4},{4,5},{5,6},{6,7},{7,0},{8,9},{9,10},{10,1... | collective-permute-start | bytes 1179656 | tf_op jit(solution)/shard_map/ppermute | solution.py:18
  187.0 19.5 %collective-permute-start.9 = (bf16[128,1536]{1,0:T(8,128)(2,1)S(1)}, bf16[128,1536]{1,0:T(8,128)(2,1)}, u32[]{:S(2)}, u32[]{:S(2)}) collective-permute-start(bf16[128,1536]{1,0:T(8,128)(2,1)S(1)} %collective-permute-done.8), channel_id=1, source_target_pairs={{0,1},{1,2},{2,3},{3,4},{4,5},{5,6},{6,7},{7,0},{8,9},{9,10},{10,1... | collective-permute-start | bytes 1179656 | tf_op jit(solution)/shard_map/ppermute | solution.py:18
  187.0 21.2 %collective-permute-start.5 = (bf16[128,1536]{1,0:T(8,128)(2,1)S(1)}, bf16[128,1536]{1,0:T(8,128)(2,1)}, u32[]{:S(2)}, u32[]{:S(2)}) collective-permute-start(bf16[128,1536]{1,0:T(8,128)(2,1)S(1)} %collective-permute-done.4), channel_id=1, source_target_pairs={{0,7},{1,0},{2,1},{3,2},{4,3},{5,4},{6,5},{7,6},{8,15},{9,8},{10,9... | collective-permute-start | bytes 1179656 | tf_op jit(solution)/shard_map/ppermute | solution.py:20
  191.0 19.9 %collective-permute-start.12 = (bf16[128,1536]{1,0:T(8,128)(2,1)S(1)}, bf16[128,1536]{1,0:T(8,128)(2,1)}, u32[]{:S(2)}, u32[]{:S(2)}) collective-permute-start(bf16[128,1536]{1,0:T(8,128)(2,1)S(1)} %collective-permute-done.11), channel_id=1, source_target_pairs={{0,7},{1,0},{2,1},{3,2},{4,3},{5,4},{6,5},{7,6},{8,15},{9,8},{10,9... | collective-permute-start | bytes 1179656 | tf_op jit(solution)/shard_map/ppermute | solution.py:20
  196.4 19.0 %collective-permute-start.2 = (bf16[128,1536]{1,0:T(8,128)(2,1)}, bf16[128,1536]{1,0:T(8,128)(2,1)}, u32[]{:S(2)}, u32[]{:S(2)}) collective-permute-start(bf16[128,1536]{1,0:T(8,128)(2,1)} %collective-permute-done.1), channel_id=1, source_target_pairs={{0,1},{1,2},{2,3},{3,4},{4,5},{5,6},{6,7},{7,0},{8,9},{9,10},{10,1... | collective-permute-start | bytes 1179656 | tf_op jit(solution)/shard_map/ppermute | solution.py:18
  206.4 17.3 %collective-permute-start.10 = (bf16[128,1536]{1,0:T(8,128)(2,1)}, bf16[128,1536]{1,0:T(8,128)(2,1)}, u32[]{:S(2)}, u32[]{:S(2)}) collective-permute-start(bf16[128,1536]{1,0:T(8,128)(2,1)} %collective-permute-done.9), channel_id=1, source_target_pairs={{0,1},{1,2},{2,3},{3,4},{4,5},{5,6},{6,7},{7,0},{8,9},{9,10},{10,1... | collective-permute-start | bytes 1179656 | tf_op jit(solution)/shard_map/ppermute | solution.py:18
  206.5 246.7 %reduce-scatter.22.cloned.1.call-start = ((), (), s32[]{:S(2)}) async-start(), calls=%async_computation.16 | async-start | bytes 3538944
  208.2 27.2 %collective-permute-start.6 = (bf16[128,1536]{1,0:T(8,128)(2,1)}, bf16[128,1536]{1,0:T(8,128)(2,1)S(1)}, u32[]{:S(2)}, u32[]{:S(2)}) collective-permute-start(bf16[128,1536]{1,0:T(8,128)(2,1)} %collective-permute-done.5), channel_id=1, source_target_pairs={{0,7},{1,0},{2,1},{3,2},{4,3},{5,4},{6,5},{7,6},{8,15},{9,8},{10,9... | collective-permute-start | bytes 1179656 | tf_op jit(solution)/shard_map/ppermute | solution.py:20
  210.9 24.4 %collective-permute-start.13 = (bf16[128,1536]{1,0:T(8,128)(2,1)}, bf16[128,1536]{1,0:T(8,128)(2,1)S(1)}, u32[]{:S(2)}, u32[]{:S(2)}) collective-permute-start(bf16[128,1536]{1,0:T(8,128)(2,1)} %collective-permute-done.12), channel_id=1, source_target_pairs={{0,7},{1,0},{2,1},{3,2},{4,3},{5,4},{6,5},{7,6},{8,15},{9,8},{10,9... | collective-permute-start | bytes 1179656 | tf_op jit(solution)/shard_map/ppermute | solution.py:20
  215.3 15.7 %collective-permute-start.3 = (bf16[128,1536]{1,0:T(8,128)(2,1)}, bf16[128,1536]{1,0:T(8,128)(2,1)S(1)}, u32[]{:S(2)}, u32[]{:S(2)}) collective-permute-start(bf16[128,1536]{1,0:T(8,128)(2,1)} %collective-permute-done.2), channel_id=1, source_target_pairs={{0,1},{1,2},{2,3},{3,4},{4,5},{5,6},{6,7},{7,0},{8,9},{9,10},{10,1... | collective-permute-start | bytes 1179656 | tf_op jit(solution)/shard_map/ppermute | solution.py:18
  392.8 110.3 %reduce-scatter.24.cloned.1.call-start = ((), (), s32[]{:S(2)}) async-start(), calls=%async_computation.17 | async-start | bytes 3538944
  407.9 217.2 %reduce-scatter.16.cloned.1.call-start = ((), (), s32[]{:S(2)}) async-start(), calls=%async_computation.13 | async-start | bytes 2433024 | tf_op jit(solution)/shard_map/reduce_scatter | solution.py:314
  411.4 338.9 %reduce-scatter.20.cloned.1.call-start = ((), (), s32[]{:S(2)}) async-start(), calls=%async_computation.15 | async-start | bytes 9732096 | tf_op jit(solution)/shard_map/reduce_scatter | solution.py:320
  419.0 471.9 %reduce-scatter.18.cloned.1.call-start = ((), (), s32[]{:S(2)}) async-start(), calls=%async_computation.14 | async-start | bytes 9732096 | tf_op jit(solution)/shard_map/reduce_scatter | solution.py:318
  426.9 589.7 %reduce-scatter.14.cloned.1.call-start = ((), (), s32[]{:S(2)}) async-start(), calls=%async_computation.12 | async-start | bytes 7299072 | tf_op jit(solution)/shard_map/reduce_scatter | solution.py:313
  509.9 719.5 %reduce-scatter.26.cloned.1.call-start = ((), (), s32[]{:S(2)}) async-start(), calls=%async_computation.18 | async-start | bytes 19464192
  (130 other events, 1781.5 us)
Sparse Core Ops, SparseCore 0:
  10.9 84.5 all-gather.5
  98.4 58.6 all-gather.7
  160.0 54.9 all-gather.9
  217.7 62.6 all-gather.11
  283.1 62.4 all-gather.13
  392.9 60.1 reduce-scatter.21
  456.9 46.2 reduce-scatter.23
  509.0 99.2 reduce-scatter.15
  615.8 134.4 reduce-scatter.19
  756.6 134.3 reduce-scatter.17
  898.2 118.3 reduce-scatter.13
  1023.4 206.0 reduce-scatter.25
